TPU v7x, 128 devices: a whole 4x4x4 slice. The times are simulated.
128 devices in a mesh: sec: 2 (over z_lo), row: 8 (over x, z_hi), col: 8 (over y, core).
Axes of the slice: x: 4, y: 4, z: 4 (z_hi: 2, z_lo: 2; z = z_hi * 2 + z_lo), core: 2. Of those that a mesh axis runs over, the one named last changes fastest.
Arguments:
- held_inverse: bfloat16 [12288, 12288], P('row', ('sec', 'col')), as said below
- factor_panels: bfloat16 [2, 12288, 1024], P(None, ('sec', 'col'), 'row'), may hold values from -0.125 to 0.125
- block_inverses: bfloat16 [2, 1024, 1024], P(None, 'row'), as said below
- covariance: float32 [12288, 12288], P('row', ('sec', 'col')), may hold values from -0.9 to 0.9
Outputs:
- updated: float32 [12288, 12288], P('row', ('sec', 'col'))
Inputs may be any that keep to these rules, and one draw needn't show every extreme that they name: held_inverse is lower triangular with a positive diagonal. Each block of block_inverses is lower triangular with a positive diagonal.
All inputs are finite; a program needn't handle non-finite values.
Results may differ from a plain program's by a relative error of at most 0.0038.
Values may be sent and summed in bfloat16 or wider, within the bound.
A program may use at most 128 MiB of HBM per device.

v0:
```python
import jax
import jax.numpy as jnp
from jax import lax
from jax.sharding import Mesh
from jax.sharding import PartitionSpec as P

PANELS = 2
ROW = ("row_0", "row_1")


def scatter_axes(x, axes, dim):
    for axis in axes:
        x = lax.psum_scatter(x, axis, scatter_dimension=dim, tiled=True)
    return x


def from_root(x, axis, root):
    mine = lax.axis_index(axis) == root
    return lax.psum(jnp.where(mine, x, jnp.zeros_like(x)), axis)


def body(held_inverse, factor_panels, block_inverses, covariance):
    total = covariance
    tile_cols = held_inverse.shape[1]
    groups = lax.axis_size(("sec", "col"))
    ratio = groups // lax.axis_size(ROW)
    column_index = lax.axis_index(("sec", "col"))
    root_row = column_index // ratio
    offset = column_index % ratio * tile_cols
    for panel in range(PANELS):
        partial_value = jnp.dot(
            factor_panels[panel], block_inverses[panel], preferred_element_type=jnp.float32
        )
        scaled = scatter_axes(partial_value, ROW, 1).astype(jnp.bfloat16)
        terms = jnp.dot(
            held_inverse,
            lax.all_gather(scaled, ROW, axis=1, tiled=True),
            preferred_element_type=jnp.float32,
        )
        summed = lax.psum(terms, ("sec", "col"))
        inverse = (-summed).astype(jnp.bfloat16)
        own_block = lax.dynamic_slice_in_dim(inverse, offset, tile_cols, 0)
        column_block = from_root(own_block, ROW, root_row)
        total = total + lax.dot_general(
            inverse, column_block, (((1,), (1,)), ((), ())), preferred_element_type=jnp.float32
        )
    return total


def solution(mesh):
    split = Mesh(
        mesh.devices.reshape(mesh.shape["sec"], 4, 2, mesh.shape["col"]),
        ("sec", "row_0", "row_1", "col"),
    )
    in_specs = (
        P(ROW, ("sec", "col")),
        P(None, ("sec", "col"), ROW),
        P(None, ROW, None),
        P(ROW, ("sec", "col")),
    )
    out_specs = P(ROW, ("sec", "col"))
    return jax.shard_map(body, mesh=split, in_specs=in_specs, out_specs=out_specs, check_vma=False)
```

profile of v0, /device:TPU:5, one launch (start us, length us, event | category | flops | bytes accessed | tf_op | source)
XLA Modules:
  0.0 585.9 jit_solution(17937898365134801965)
XLA Ops:
  6.5 0.0 copy-start
  6.5 0.0 copy-start.4
  6.5 0.0 copy-start.5
  6.5 0.0 reduce-scatter.5.cloned.1.call-start
  6.5 3.4 fusion.2
  10.0 0.0 reduce-scatter.5.cloned.1.call-update
  10.0 0.0 reduce-scatter.9.cloned.1.call-start
  10.0 0.0 copy-done.4
  10.0 0.0 copy-done.5
  10.1 2.2 fusion
  12.3 0.0 reduce-scatter.9.cloned.1.call-update
  12.3 0.0 reduce-scatter.7.cloned.1.call-start
  12.3 36.8 %reduce-scatter.5.cloned.1.call-done = f32[768,256]{1,0:T(8,128)} async-done(((f32[768,1024]{1,0:T(8,128)}), f32[768,256]{1,0:T(8,128)}) %reduce-scatter.5.cloned.1.call-update) | async-done | bytes 786448 | tf_op jit(solution)/shard_map/reduce_scatter | solution.py:13
  49.2 0.0 reduce-scatter.7.cloned.1.call-update
  49.2 0.0 reduce-scatter.11.cloned.1.call-start
  49.2 40.3 %reduce-scatter.9.cloned.1.call-done = f32[768,256]{1,0:T(8,128)} async-done(((f32[768,1024]{1,0:T(8,128)}), f32[768,256]{1,0:T(8,128)}) %reduce-scatter.9.cloned.1.call-update) | async-done | bytes 786448 | tf_op jit(solution)/shard_map/reduce_scatter | solution.py:13
  89.6 0.0 reduce-scatter.11.cloned.1.call-update
  89.6 0.0 all-gather.3.cloned.1.call-start
  89.6 25.2 %reduce-scatter.7.cloned.1.call-done = f32[768,128]{1,0:T(8,128)} async-done(((f32[768,256]{1,0:T(8,128)}), f32[768,128]{1,0:T(8,128)}) %reduce-scatter.7.cloned.1.call-update) | async-done | bytes 393232 | tf_op jit(solution)/shard_map/reduce_scatter | solution.py:13
  114.8 1.7 convert_element_type.12
  116.5 0.0 all-gather.3.cloned.1.call-update
  116.6 0.0 all-gather.5.cloned.1.call-start
  116.6 21.3 %reduce-scatter.11.cloned.1.call-done = f32[768,128]{1,0:T(8,128)} async-done(((f32[768,256]{1,0:T(8,128)}), f32[768,128]{1,0:T(8,128)}) %reduce-scatter.11.cloned.1.call-update) | async-done | bytes 393232 | tf_op jit(solution)/shard_map/reduce_scatter | solution.py:13
  138.0 1.7 convert_element_type.14
  139.7 0.0 all-gather.5.cloned.1.call-update
  139.7 0.0 all-reduce.5.cloned.1.call-start
  139.7 49.3 %all-gather.3.cloned.1.call-done = bf16[768,1024]{1,0:T(8,128)(2,1)} async-done(((bf16[768,128]{1,0:T(8,128)(2,1)}), bf16[768,1024]{1,0:T(8,128)(2,1)}) %all-gather.3.cloned.1.call-update) | async-done | bytes 1572880 | tf_op jit(solution)/shard_map/all_gather | solution.py:37
  189.0 0.0 copy-done
  189.0 6.1 %convolution_bitcast_fusion.1 = f32[1536,1024]{0,1:T(8,128)} fusion(bf16[768,1024]{1,0:T(8,128)(2,1)} %all-gather.3.cloned.1.call-done, bf16[1536,768]{1,0:T(8,128)(2,1)S(1)} %copy-done), kind=kOutput, calls=%fused_computation.4 | convolution fusion | flops 2415919104 | bytes 10223616 | tf_op jit(solution)/shard_map/dot_general | solution.py:35
  195.2 47.0 %all-gather.5.cloned.1.call-done = bf16[768,1024]{1,0:T(8,128)(2,1)} async-done(((bf16[768,128]{1,0:T(8,128)(2,1)}), bf16[768,1024]{1,0:T(8,128)(2,1)}) %all-gather.5.cloned.1.call-update) | async-done | bytes 1572880 | tf_op jit(solution)/shard_map/all_gather | solution.py:37
  242.1 6.0 %convolution_bitcast_fusion = f32[1536,1024]{0,1:T(8,128)} fusion(bf16[768,1024]{1,0:T(8,128)(2,1)} %all-gather.5.cloned.1.call-done, bf16[1536,768]{1,0:T(8,128)(2,1)S(1)} %copy-done), kind=kOutput, calls=%fused_computation.3 | convolution fusion | flops 2415919104 | bytes 10223616 | tf_op jit(solution)/shard_map/dot_general | solution.py:35
  248.1 0.0 all-reduce.5.cloned.1.call-update
  248.1 0.0 all-reduce.7.cloned.1.call-start
  248.2 159.2 %all-reduce.5.cloned.1.call-done = (f32[1536,1024]{0,1:T(8,128)}, f32[1536,1024]{0,1:T(8,128)}) async-done(((f32[1536,1024]{0,1:T(8,128)}, f32[1536,1024]{0,1:T(8,128)}), (f32[1536,1024]{0,1:T(8,128)}, f32[1536,1024]{0,1:T(8,128)})) %all-reduce.5.cloned.1.call-update) | async-done | bytes 12582928 | tf_op jit(solution)/shard_map/psum | solution.py:40
  407.4 6.3 %negate_convert_fusion = (bf16[1536,1024]{0,1:T(8,128)(2,1)S(1)}, bf16[1536,1024]{0,1:T(8,128)(2,1)S(1)}) fusion(f32[1536,1024]{0,1:T(8,128)} %get-tuple-element.6, f32[1536,1024]{0,1:T(8,128)} %get-tuple-element.5), kind=kLoop, calls=%fused_computation | loop fusion | flops 6291456 | bytes 18874368 | tf_op jit(solution)/shard_map/convert_element_type | solution.py:41
  413.7 0.0 copy-start.2
  413.7 1.7 dynamic-slice_select_fusion.1
  415.4 0.4 copy-done.2
  415.9 1.5 dynamic-slice_select_fusion
  417.4 0.0 all-reduce.7.cloned.1.call-update
  417.4 151.0 %all-reduce.7.cloned.1.call-done = (bf16[768,1024]{0,1:T(8,128)(2,1)}, bf16[768,1024]{0,1:T(8,128)(2,1)}) async-done(((bf16[768,1024]{0,1:T(8,128)(2,1)}, bf16[768,1024]{0,1:T(8,128)(2,1)}), (bf16[768,1024]{0,1:T(8,128)(2,1)}, bf16[768,1024]{0,1:T(8,128)(2,1)})) %all-reduce.7.cloned.1.call-update) | async-done | bytes 3145744 | tf_op jit(solution)/shard_map/psum | solution.py:19
  568.4 0.0 copy-start.3
  568.4 0.0 copy-start.6
  568.4 4.3 fusion.10
  572.7 0.0 copy-done.3
  572.7 0.0 copy-done.6
  572.7 0.0 copy-start.1
  572.7 6.4 %add_add_fusion = f32[1536,768]{1,0:T(8,128)} fusion(f32[1536,768]{1,0:T(8,128)} %param.7, f32[1536,768]{1,0:T(8,128)S(1)} %fusion.10, bf16[1536,1024]{0,1:T(8,128)(2,1)S(1)} %copy-done.3, bf16[768,1024]{0,1:T(8,128)(2,1)S(1)} %copy-done.6), kind=kOutput, calls=%fused_computation.2 | convolution fusion | flops 2418278400 | bytes 18874368 | tf_op jit(solution)/shard_map/dot_general | solution.py:44
  579.1 0.0 copy-done.1
Async XLA Ops:
  6.5 182.5 %copy-start = (bf16[1536,768]{1,0:T(8,128)(2,1)S(1)}, bf16[1536,768]{1,0:T(8,128)(2,1)}, u32[]{:S(2)}) copy-start(bf16[1536,768]{1,0:T(8,128)(2,1)} %param.4) | copy-start | bytes 7077892
  6.5 3.5 copy-start.4
  6.5 3.5 copy-start.5
  6.5 42.6 %reduce-scatter.5.cloned.1.call-start = ((), (), s32[]{:S(2)}) async-start(), calls=%async_computation.4 | async-start | bytes 3932160 | tf_op jit(solution)/shard_map/reduce_scatter | solution.py:13
  10.0 79.6 %reduce-scatter.9.cloned.1.call-start = ((), (), s32[]{:S(2)}) async-start(), calls=%async_computation.7 | async-start | bytes 3932160 | tf_op jit(solution)/shard_map/reduce_scatter | solution.py:13
  12.3 102.6 %reduce-scatter.7.cloned.1.call-start = ((), (), s32[]{:S(2)}) async-start(), calls=%async_computation.5 | async-start | bytes 1179648 | tf_op jit(solution)/shard_map/reduce_scatter | solution.py:13
  49.2 88.8 %reduce-scatter.11.cloned.1.call-start = ((), (), s32[]{:S(2)}) async-start(), calls=%async_computation.8 | async-start | bytes 1179648 | tf_op jit(solution)/shard_map/reduce_scatter | solution.py:13
  89.6 99.4 %all-gather.3.cloned.1.call-start = ((), (), s32[]{:S(2)}) async-start(), calls=%async_computation.6 | async-start | bytes 1769472 | tf_op jit(solution)/shard_map/all_gather | solution.py:37
  116.6 125.6 %all-gather.5.cloned.1.call-start = ((), (), s32[]{:S(2)}) async-start(), calls=%async_computation.9 | async-start | bytes 1769472 | tf_op jit(solution)/shard_map/all_gather | solution.py:37
  139.7 267.7 %all-reduce.5.cloned.1.call-start = ((), (), s32[]{:S(2)}) async-start(), calls=%async_computation.10 | async-start | bytes 25165824 | tf_op jit(solution)/shard_map/psum | solution.py:40
  248.1 320.3 %all-reduce.7.cloned.1.call-start = ((), (), s32[]{:S(2)}) async-start(), calls=%async_computation.11 | async-start | bytes 6291456 | tf_op jit(solution)/shard_map/psum | solution.py:19
  413.7 2.2 copy-start.2
  568.4 4.3 copy-start.3
  568.4 4.3 copy-start.6
  572.7 6.4 %copy-start.1 = (bf16[1536,768]{1,0:T(8,128)(2,1)S(1)}, bf16[1536,768]{1,0:T(8,128)(2,1)}, u32[]{:S(2)}) copy-start(bf16[1536,768]{1,0:T(8,128)(2,1)} %param.4) | copy-start | bytes 7077892
Sparse Core Ops, SparseCore 0:
  10.1 38.9 reduce-scatter.4
  51.6 37.9 reduce-scatter.8
  91.9 22.8 reduce-scatter.6
  117.0 20.8 reduce-scatter.10
  140.0 48.9 all-gather.2
  191.0 51.0 all-gather.4
  248.2 159.1 all-reduce.4
  417.5 150.8 all-reduce.6
where the time goes:
time: 586 us
  waiting for transfers between devices  530 us (90%)
  matrix products  28.4 us (5%)
  between operations  13.6 us (2%)
  other arithmetic  12.9 us (2%)
    psum x1, waiting for transfers between devices, body(): summed = lax.psum(terms, ('sec', 'col'))  159 us
    psum x1, waiting for transfers between devices, from_root(): return lax.psum(jnp.where(mine, x, jnp.zeros_like(x)), axis)  151 us
    reduce_scatter x4, waiting for transfers between devices, scatter_axes(): x = lax.psum_scatter(x, axis, scatter_dimension=dim, tiled=True)  124 us
    all_gather x2, waiting for transfers between devices, body(): lax.all_gather(scaled, ROW, axis=1, tiled=True)  96.2 us
    dot_general x2, matrix products, body(): jnp.dot(held_inverse, lax.all_gather(scaled, ROW, axis=1, tiled=True), pr...  12.1 us
  transfers between devices with their start and end apart: 8, of which 8 were waited for; matrix products, arithmetic and copies ran while one was open for 2% of the time, Pallas kernels for 0%

commit v1 on v0

--- a/solution.py
+++ b/solution.py
@@ -37,7 +37,7 @@
             lax.all_gather(scaled, ROW, axis=1, tiled=True),
             preferred_element_type=jnp.float32,
         )
-        summed = lax.psum(terms, ("sec", "col"))
+        summed = lax.psum(lax.psum(terms, axis_name="col"), axis_name="sec")
         inverse = (-summed).astype(jnp.bfloat16)
         own_block = lax.dynamic_slice_in_dim(inverse, offset, tile_cols, 0)
         column_block = from_root(own_block, ROW, root_row)

time: 586 us -> 869 us (1.48)
  waiting for transfers between devices: 530 us -> 814 us
    psum x1 -> x2, waiting for transfers between devices: 159 us -> 442 us  [body(): summed = lax.psum(lax.psum(terms, axis_name='col'), axis_name='sec')]
  transfers between devices with their start and end apart: 8 -> 9, of which waited for: 8 -> 9; matrix products, arithmetic and copies ran while one was open for 2% -> 1% of each run, Pallas kernels for 0% -> 0%
where the time goes in v1:
time: 869 us
  waiting for transfers between devices  814 us (94%)
  matrix products  28.4 us (3%)
  between operations  13.3 us (2%)
  other arithmetic  12.9 us (1%)
    psum x2, waiting for transfers between devices, body(): summed = lax.psum(lax.psum(terms, axis_name='col'), axis_name='sec')  442 us
    psum x1, waiting for transfers between devices, from_root(): return lax.psum(jnp.where(mine, x, jnp.zeros_like(x)), axis)  151 us
    reduce_scatter x4, waiting for transfers between devices, scatter_axes(): x = lax.psum_scatter(x, axis, scatter_dimension=dim, tiled=True)  124 us
    all_gather x2, waiting for transfers between devices, body(): lax.all_gather(scaled, ROW, axis=1, tiled=True)  96.3 us
  transfers between devices with their start and end apart: 9, of which 9 were waited for; matrix products, arithmetic and copies ran while one was open for 1% of the time, Pallas kernels for 0%

profile of v1, /device:TPU:5, one launch (start us, length us, event | category | flops | bytes accessed | tf_op | source)
XLA Modules:
  0.0 869.1 jit_solution(11526498549195027710)
XLA Ops:
  6.5 0.0 copy-start
  6.5 0.0 copy-start.4
  6.5 0.0 copy-start.5
  6.5 0.0 reduce-scatter.5.cloned.1.call-start
  6.5 3.4 fusion.2
  10.0 0.0 reduce-scatter.5.cloned.1.call-update
  10.0 0.0 reduce-scatter.9.cloned.1.call-start
  10.0 0.0 copy-done.4
  10.0 0.0 copy-done.5
  10.1 2.2 fusion
  12.3 0.0 reduce-scatter.9.cloned.1.call-update
  12.3 0.0 reduce-scatter.7.cloned.1.call-start
  12.3 36.8 %reduce-scatter.5.cloned.1.call-done = f32[768,256]{1,0:T(8,128)} async-done(((f32[768,1024]{1,0:T(8,128)}), f32[768,256]{1,0:T(8,128)}) %reduce-scatter.5.cloned.1.call-update) | async-done | bytes 786448 | tf_op jit(solution)/shard_map/reduce_scatter | solution.py:13
  49.2 0.0 reduce-scatter.7.cloned.1.call-update
  49.2 0.0 reduce-scatter.11.cloned.1.call-start
  49.2 40.3 %reduce-scatter.9.cloned.1.call-done = f32[768,256]{1,0:T(8,128)} async-done(((f32[768,1024]{1,0:T(8,128)}), f32[768,256]{1,0:T(8,128)}) %reduce-scatter.9.cloned.1.call-update) | async-done | bytes 786448 | tf_op jit(solution)/shard_map/reduce_scatter | solution.py:13
  89.6 0.0 reduce-scatter.11.cloned.1.call-update
  89.6 0.0 all-gather.3.cloned.1.call-start
  89.6 25.2 %reduce-scatter.7.cloned.1.call-done = f32[768,128]{1,0:T(8,128)} async-done(((f32[768,256]{1,0:T(8,128)}), f32[768,128]{1,0:T(8,128)}) %reduce-scatter.7.cloned.1.call-update) | async-done | bytes 393232 | tf_op jit(solution)/shard_map/reduce_scatter | solution.py:13
  114.8 1.7 convert_element_type.12
  116.5 0.0 all-gather.3.cloned.1.call-update
  116.6 0.0 all-gather.5.cloned.1.call-start
  116.6 21.3 %reduce-scatter.11.cloned.1.call-done = f32[768,128]{1,0:T(8,128)} async-done(((f32[768,256]{1,0:T(8,128)}), f32[768,128]{1,0:T(8,128)}) %reduce-scatter.11.cloned.1.call-update) | async-done | bytes 393232 | tf_op jit(solution)/shard_map/reduce_scatter | solution.py:13
  138.0 1.7 convert_element_type.14
  139.7 0.0 all-gather.5.cloned.1.call-update
  139.7 0.0 all-reduce.7.cloned.1.call-start
  139.7 49.3 %all-gather.3.cloned.1.call-done = bf16[768,1024]{1,0:T(8,128)(2,1)} async-done(((bf16[768,128]{1,0:T(8,128)(2,1)}), bf16[768,1024]{1,0:T(8,128)(2,1)}) %all-gather.3.cloned.1.call-update) | async-done | bytes 1572880 | tf_op jit(solution)/shard_map/all_gather | solution.py:37
  189.0 0.0 copy-done
  189.0 6.0 convolution_bitcast_fusion.1
  195.0 47.1 %all-gather.5.cloned.1.call-done = bf16[768,1024]{1,0:T(8,128)(2,1)} async-done(((bf16[768,128]{1,0:T(8,128)(2,1)}), bf16[768,1024]{1,0:T(8,128)(2,1)}) %all-gather.5.cloned.1.call-update) | async-done | bytes 1572880 | tf_op jit(solution)/shard_map/all_gather | solution.py:37
  242.1 6.1 convolution_bitcast_fusion
  248.2 0.0 all-reduce.7.cloned.1.call-update
  248.2 0.0 all-reduce.9.cloned.1.call-start
  248.3 144.9 %all-reduce.7.cloned.1.call-done = (f32[1536,1024]{0,1:T(8,128)}, f32[1536,1024]{0,1:T(8,128)}) async-done(((f32[1536,1024]{0,1:T(8,128)}, f32[1536,1024]{0,1:T(8,128)}), (f32[1536,1024]{0,1:T(8,128)}, f32[1536,1024]{0,1:T(8,128)})) %all-reduce.7.cloned.1.call-update) | async-done | bytes 12582928 | tf_op jit(solution)/shard_map/psum | solution.py:40
  393.2 0.0 all-reduce.9.cloned.1.call-update
  393.2 0.0 all-reduce.11.cloned.1.call-start
  393.3 297.4 %all-reduce.9.cloned.1.call-done = (f32[1536,1024]{0,1:T(8,128)}, f32[1536,1024]{0,1:T(8,128)}) async-done(((f32[1536,1024]{0,1:T(8,128)}, f32[1536,1024]{0,1:T(8,128)}), (f32[1536,1024]{0,1:T(8,128)}, f32[1536,1024]{0,1:T(8,128)})) %all-reduce.9.cloned.1.call-update) | async-done | bytes 12582928 | tf_op jit(solution)/shard_map/psum | solution.py:40
  690.7 6.3 negate_convert_fusion
  697.0 0.0 copy-start.2
  697.0 1.7 dynamic-slice_select_fusion.1
  698.7 0.4 copy-done.2
  699.2 1.5 dynamic-slice_select_fusion
  700.7 0.0 all-reduce.11.cloned.1.call-update
  700.7 151.2 %all-reduce.11.cloned.1.call-done = (bf16[768,1024]{0,1:T(8,128)(2,1)}, bf16[768,1024]{0,1:T(8,128)(2,1)}) async-done(((bf16[768,1024]{0,1:T(8,128)(2,1)}, bf16[768,1024]{0,1:T(8,128)(2,1)}), (bf16[768,1024]{0,1:T(8,128)(2,1)}, bf16[768,1024]{0,1:T(8,128)(2,1)})) %all-reduce.11.cloned.1.call-update) | async-done | bytes 3145744 | tf_op jit(solution)/shard_map/psum | solution.py:19
  851.9 0.0 copy-start.3
  851.9 0.0 copy-start.6
  851.9 4.3 fusion.10
  856.2 0.0 copy-done.3
  856.2 0.0 copy-done.6
  856.2 0.0 copy-start.1
  856.2 6.4 add_add_fusion
  862.6 0.0 copy-done.1
Async XLA Ops:
  6.5 182.5 %copy-start = (bf16[1536,768]{1,0:T(8,128)(2,1)S(1)}, bf16[1536,768]{1,0:T(8,128)(2,1)}, u32[]{:S(2)}) copy-start(bf16[1536,768]{1,0:T(8,128)(2,1)} %param.4) | copy-start | bytes 7077892
  6.5 3.5 copy-start.4
  6.5 3.5 copy-start.5
  6.5 42.6 %reduce-scatter.5.cloned.1.call-start = ((), (), s32[]{:S(2)}) async-start(), calls=%async_computation.4 | async-start | bytes 3932160 | tf_op jit(solution)/shard_map/reduce_scatter | solution.py:13
  10.0 79.6 %reduce-scatter.9.cloned.1.call-start = ((), (), s32[]{:S(2)}) async-start(), calls=%async_computation.7 | async-start | bytes 3932160 | tf_op jit(solution)/shard_map/reduce_scatter | solution.py:13
  12.3 102.6 %reduce-scatter.7.cloned.1.call-start = ((), (), s32[]{:S(2)}) async-start(), calls=%async_computation.5 | async-start | bytes 1179648 | tf_op jit(solution)/shard_map/reduce_scatter | solution.py:13
  49.2 88.8 %reduce-scatter.11.cloned.1.call-start = ((), (), s32[]{:S(2)}) async-start(), calls=%async_computation.8 | async-start | bytes 1179648 | tf_op jit(solution)/shard_map/reduce_scatter | solution.py:13
  89.6 99.4 %all-gather.3.cloned.1.call-start = ((), (), s32[]{:S(2)}) async-start(), calls=%async_computation.6 | async-start | bytes 1769472 | tf_op jit(solution)/shard_map/all_gather | solution.py:37
  116.6 125.6 %all-gather.5.cloned.1.call-start = ((), (), s32[]{:S(2)}) async-start(), calls=%async_computation.9 | async-start | bytes 1769472 | tf_op jit(solution)/shard_map/all_gather | solution.py:37
  139.7 253.5 %all-reduce.7.cloned.1.call-start = ((), (), s32[]{:S(2)}) async-start(), calls=%async_computation.10 | async-start | bytes 25165824 | tf_op jit(solution)/shard_map/psum | solution.py:40
  248.2 442.5 %all-reduce.9.cloned.1.call-start = ((), (), s32[]{:S(2)}) async-start(), calls=%async_computation.11 | async-start | bytes 25165824 | tf_op jit(solution)/shard_map/psum | solution.py:40
  393.2 458.7 %all-reduce.11.cloned.1.call-start = ((), (), s32[]{:S(2)}) async-start(), calls=%async_computation.12 | async-start | bytes 6291456 | tf_op jit(solution)/shard_map/psum | solution.py:19
  697.0 2.2 copy-start.2
  851.9 4.3 copy-start.3
  851.9 4.4 copy-start.6
  856.2 6.4 copy-start.1
Sparse Core Ops, SparseCore 0:
  10.1 38.9 reduce-scatter.4
  51.6 37.9 reduce-scatter.8
  91.9 22.8 reduce-scatter.6
  117.0 20.8 reduce-scatter.10
  140.0 48.9 all-gather.2
  191.0 51.0 all-gather.4
  248.3 144.8 all-reduce.6
  395.8 294.8 all-reduce.8
  700.8 151.0 all-reduce.10
